TPU v7x, 32 devices: a whole 2x2x4 slice. The times are simulated.
32 devices in a mesh: energy: 16 (over z, y, x), slab: 2 (over core).
Axes of the slice: x: 2, y: 2, z: 4, core: 2. Of those that a mesh axis runs over, the one named last changes fastest.
Arguments:
- g_less: bfloat16 [1024, 2, 5, 64, 128], P('energy', 'slab'), may hold values from -6 to 6
- g_greater: bfloat16 [1024, 2, 5, 64, 128], P('energy', 'slab'), may hold values from -6 to 6
- coulomb: bfloat16 [2, 64, 192], P('slab'), may hold values from -0.4375 to 0.4375
- pattern: int32 [2, 5], replicated, may hold values from 0 to 7, as said below
Outputs:
- screened: bfloat16 [1024, 2, 5, 64, 128], P('energy', 'slab')
Inputs may be any that keep to these rules, and one draw needn't show every extreme that they name: `pattern`: row r holds 5 distinct columns: r, r + 3, r + 6 and two of r + 1, r + 2, r + 4, r + 5, in any order of slots.
All inputs are finite; a program needn't handle non-finite values.
Results may differ from a plain program's by a relative error of at most 0.007.
Values may be sent and summed in bfloat16 or wider, within the bound.
A program may use at most 128 MiB of HBM per device.

v0:
```python
import functools
import math

import jax
import jax.numpy as jnp
import numpy as np
from jax import lax
from jax.experimental import pallas as pl
from jax.experimental.pallas import tpu as pltpu
from jax.sharding import PartitionSpec as P

MESH = pl.DeviceIdType.MESH
LANES = 128


def make_tables(count):
    index = np.arange(count)
    angles = (index[:, None] * index[None, :] % count) * (2.0 * math.pi / count)
    scale = 1.0 / math.sqrt(count)
    table_real = (np.cos(angles) * scale).astype(np.float32).astype(jnp.bfloat16)
    table_imag = (-np.sin(angles) * scale).astype(np.float32).astype(jnp.bfloat16)
    return table_real, table_imag


def split_tables(count, radix):
    part = count // radix
    cut = np.stack(make_tables(count))[:, :part, :].reshape(2, part, part, radix)
    return np.ascontiguousarray(cut.transpose(0, 3, 1, 2)), np.ascontiguousarray(cut.transpose(0, 3, 2, 1))


def turn(values, sign):
    return sign * pltpu.roll(values, LANES // 2, 1)


def exchange_kernel(
    peers, count, radix, less_hbm, great_hbm, coulomb_ref, fwd_ref, inv_ref,
    own_hbm, below_hbm, above_hbm,
    stage, send, held, reply, back_ref, result, lhs, shared,
    load_sem, send_sem, recv_sem, back_send, back_recv,
    own_sem, edge_send, edge_recv, lhs_send, lhs_recv,
):
    me = lax.axis_index("energy")
    row = lax.axis_index("slab")
    has_below, has_above = row > 0, row < count - 1
    slots = send.shape[1]
    local = send.shape[4]
    wide = send.shape[5]
    quads = wide // LANES
    part = held.shape[3]
    slot_rows = stage.shape[3]

    barrier = pltpu.get_barrier_semaphore()

    def greet(step, carry):
        peer = lax.rem(me + step, peers)
        pl.semaphore_signal(barrier, inc=1, device_id={"energy": peer}, device_id_type=MESH)
        return carry

    def load(which, slot, buf):
        source = (less_hbm, great_hbm)[which]
        return pltpu.make_async_copy(source.at[:, :, slot], stage.at[buf], load_sem.at[buf])

    load(0, 0, 0).start()
    lax.fori_loop(1, peers, greet, 0)
    links = ((has_above, row + 1), (has_below, row - 1)) if count > 1 else ()
    for there, peer in links:
        @pl.when(there)
        def _(peer=peer):
            pl.semaphore_signal(barrier, inc=1, device_id={"slab": peer}, device_id_type=MESH)
    greeted = peers - 1
    for there, _ in links:
        greeted = greeted + there.astype(jnp.int32)

    lane = lax.broadcasted_iota(jnp.int32, (1, LANES), 1)
    sign = jnp.where(lane < LANES // 2, -1.0, 1.0).astype(jnp.float32)

    def scatter(which, slot):
        load(which, slot, which).wait()
        if which == 0:
            load(1, slot, 1).start()
        else:
            @pl.when(slot + 1 < slots)
            def _():
                load(0, slot + 1, 0).start()

        def cut(group, carry):
            top = pl.multiple_of(group * 8, 8)
            for r in range(radix):
                tile = stage[which, :, r, pl.ds(top, 8), :].astype(jnp.float32)
                tile = jnp.swapaxes(tile, 0, 1).astype(jnp.bfloat16)
                for k in range(8):
                    send[which, slot, group * (8 // quads) + k // quads, r, :,
                         (k % quads) * LANES : (k % quads + 1) * LANES] = tile[k]
            return carry

        lax.fori_loop(0, slot_rows // 8, cut, 0)
        if which == 0:
            @pl.when(slot == 0)
            def _():
                pl.semaphore_wait(barrier, greeted)

        rows = pl.ds(pl.multiple_of(me * local, local), local)
        pltpu.make_async_copy(
            send.at[which, slot, me], held.at[which, slot, :, rows, :], recv_sem.at[which, slot]
        ).start()

        def ship(step, carry):
            peer = lax.rem(me + peers // 2 + step, peers)

            @pl.when(peer != me)
            def _():
                pltpu.make_async_remote_copy(
                    src_ref=send.at[which, slot, peer],
                    dst_ref=held.at[which, slot, :, rows, :],
                    send_sem=send_sem.at[which, slot],
                    recv_sem=recv_sem.at[which, slot],
                    device_id={"energy": peer},
                    device_id_type=MESH,
                ).start()
            return carry

        lax.fori_loop(0, peers, ship, 0)

    def scatter_slot(slot, carry):
        scatter(0, slot)
        scatter(1, slot)
        return carry

    lax.fori_loop(0, slots, scatter_slot, 0)

    orbitals = coulomb_ref.shape[0]
    entry = lax.broadcasted_iota(jnp.int32, (3 * orbitals, orbitals), 0)
    place = lax.broadcasted_iota(jnp.int32, (3 * orbitals, orbitals), 1)
    wanted = lax.rem(place, peers) * quads + place // peers
    for d in range(3):
        select = (entry == wanted + d * orbitals).astype(jnp.float32).astype(jnp.bfloat16)
        block = jnp.dot(coulomb_ref[...], select, preferred_element_type=jnp.float32)
        shared[d] = block.astype(jnp.bfloat16)
    lhs[0] = shared[1]

    def lend(side):
        block, peer = ((2, row + 1), (0, row - 1))[side]
        return pltpu.make_async_remote_copy(
            src_ref=shared.at[block],
            dst_ref=lhs.at[2 - side],
            send_sem=lhs_send.at[side],
            recv_sem=lhs_recv.at[2 - side],
            device_id={"slab": peer},
            device_id_type=MESH,
        )

    for side, (there, _) in enumerate(links):
        @pl.when(there)
        def _(side=side):
            lend(side).start()

    def forward(which, slot, col):
        pieces = []
        for r in range(radix):
            block = held[which, slot, r, :, col]
            direct = jnp.dot(fwd_ref[0, r], block, preferred_element_type=jnp.float32)
            crossed = jnp.dot(fwd_ref[1, r], block, preferred_element_type=jnp.float32)
            pieces.append(direct + turn(crossed, sign))
        if radix == 1:
            return pieces
        even, odd = pieces[0] + pieces[2], pieces[1] + pieces[3]
        gap, twist = pieces[0] - pieces[2], turn(pieces[1] - pieces[3], sign)
        return [even + odd, gap - twist, even - odd, gap + twist]

    def compute(slot, carry):
        for which in range(2):
            pltpu.make_async_copy(
                held.at[which, slot], held.at[which, slot], recv_sem.at[which, slot]
            ).wait()
        for quad in range(quads):
            col = slice(quad * LANES, (quad + 1) * LANES)
            lesser = forward(0, slot, col)
            greater = forward(1, slot, col)
            products = []
            for a, b in zip(lesser, greater):
                along = a * b
                across = a * pltpu.roll(b, LANES // 2, 1)
                products.append(
                    jnp.where(
                        lane < LANES // 2,
                        along + pltpu.roll(along, LANES // 2, 1),
                        across - pltpu.roll(across, LANES // 2, 1),
                    )
                )
            if radix == 4:
                z0, z1, z2, z3 = products
                even, odd = z0 + z2, z1 + z3
                gap, twist = z0 - z2, turn(z1 - z3, sign)
                products = [even + odd, gap + twist, even - odd, gap - twist]
            for r in range(radix):
                block = products[r].astype(jnp.bfloat16)
                direct = jnp.dot(inv_ref[0, r], block, preferred_element_type=jnp.float32)
                crossed = jnp.dot(inv_ref[1, r], block, preferred_element_type=jnp.float32)
                reply[slot, r, :, col] = (direct - turn(crossed, sign)).astype(jnp.bfloat16)

        own = pl.ds(pl.multiple_of(me * local, local), local)
        pltpu.make_async_copy(
            reply.at[slot, :, own, :], back_ref.at[slot, me], back_recv.at[slot]
        ).start()

        def ship(step, carry):
            peer = lax.rem(me + peers // 2 + step, peers)
            rows = pl.ds(pl.multiple_of(peer * local, local), local)

            @pl.when(peer != me)
            def _():
                pltpu.make_async_remote_copy(
                    src_ref=reply.at[slot, :, rows, :],
                    dst_ref=back_ref.at[slot, me],
                    send_sem=back_send.at[slot],
                    recv_sem=back_recv.at[slot],
                    device_id={"energy": peer},
                    device_id_type=MESH,
                ).start()
            return carry

        lax.fori_loop(0, peers, ship, 0)
        return carry

    lax.fori_loop(0, slots, compute, 0)

    for side, (there, _) in enumerate(links):
        @pl.when(there)
        def _(side=side):
            lend(side).wait_send()
            pltpu.make_async_copy(lhs.at[1 + side], lhs.at[1 + side], lhs_recv.at[1 + side]).wait()

        @pl.when(jnp.logical_not(there))
        def _(side=side):
            lhs[1 + side] = jnp.zeros(lhs.shape[1:], lhs.dtype)

    def hand(side, slot):
        peer = (row + 1, row - 1)[side]
        target = (below_hbm, above_hbm)[side]
        return pltpu.make_async_remote_copy(
            src_ref=result.at[1 + side, slot],
            dst_ref=target.at[slot],
            send_sem=edge_send.at[side, slot],
            recv_sem=edge_recv.at[side, slot],
            device_id={"slab": peer},
            device_id_type=MESH,
        )

    def keep(slot):
        return pltpu.make_async_copy(result.at[0, slot], own_hbm.at[slot], own_sem.at[slot])

    def screen(slot, carry):
        pltpu.make_async_copy(back_ref.at[slot], back_ref.at[slot], back_recv.at[slot]).wait()
        left = jnp.concatenate([lhs[0], lhs[1], lhs[2]], 0)

        def energies(r, inner):
            rows = []
            for quad in range(quads):
                tile = back_ref[slot, :, r, :, quad * LANES : (quad + 1) * LANES]
                tile = jnp.swapaxes(tile.astype(jnp.float32), 0, 1)
                rows.append(tile.astype(jnp.bfloat16))
            right = jnp.concatenate(rows, 1)
            for e in range(local):
                both = jnp.dot(left, right[e], preferred_element_type=jnp.float32)
                for k in range(3):
                    part_of = both[k * orbitals : (k + 1) * orbitals]
                    result[k, slot, e, r] = part_of.astype(jnp.bfloat16)
            return inner

        lax.fori_loop(0, radix, energies, 0)
        for side, (there, _) in enumerate(links):
            @pl.when(there)
            def _(side=side):
                hand(side, slot).start()
        keep(slot).start()
        return carry

    lax.fori_loop(0, slots, screen, 0)

    def finish(slot, carry):
        rest = pl.ds(0, peers - 1)
        for which in range(2):
            pltpu.make_async_copy(
                send.at[which, slot, rest], send.at[which, slot, rest], send_sem.at[which, slot]
            ).wait()
        pltpu.make_async_copy(
            send.at[0, slot, rest], send.at[0, slot, rest], back_send.at[slot]
        ).wait()
        keep(slot).wait()
        for side, (there, _) in enumerate(links):
            @pl.when(there)
            def _(side=side):
                hand(side, slot).wait_send()
        for side, there in enumerate((has_below, has_above)) if count > 1 else ():
            target = (below_hbm, above_hbm)[side]

            @pl.when(there)
            def _(side=side, target=target):
                pltpu.make_async_copy(
                    target.at[slot], target.at[slot], edge_recv.at[side, slot]
                ).wait()
        return carry

    lax.fori_loop(0, slots, finish, 0)


def polarization(g_less, g_greater, coulomb):
    e_local, _, slots, orbitals, cols = g_less.shape
    peers, rows = lax.axis_size("energy"), lax.axis_size("slab")
    count = e_local * peers
    radix = 4 if e_local % 64 == 0 else 1
    part = count // radix
    local = e_local // radix
    wide = orbitals // peers * cols
    forward, inverse = split_tables(count, radix)
    shape = (local, radix, slots, orbitals, cols)
    anywhere = pl.BlockSpec(memory_space=pl.ANY)
    vmem = pl.BlockSpec(memory_space=pltpu.VMEM)
    bf16 = jnp.bfloat16
    dma = pltpu.SemaphoreType.DMA
    return pl.pallas_call(
        functools.partial(exchange_kernel, peers, rows, radix),
        out_shape=[jax.ShapeDtypeStruct((slots, local, radix, orbitals, cols), bf16)] * 3,
        in_specs=[anywhere, anywhere, vmem, vmem, vmem],
        out_specs=[anywhere] * 3,
        scratch_shapes=[
            pltpu.VMEM((2, local, radix, orbitals, cols), bf16),
            pltpu.VMEM((2, slots, peers, radix, local, wide), bf16),
            pltpu.VMEM((2, slots, radix, part, wide), bf16),
            pltpu.VMEM((slots, radix, part, wide), bf16),
            pltpu.VMEM((slots, peers, radix, local, wide), bf16),
            pltpu.VMEM((3, slots, local, radix, orbitals, cols), bf16),
            pltpu.VMEM((3, orbitals, orbitals), bf16),
            pltpu.VMEM((3, orbitals, orbitals), bf16),
            dma((2,)), dma((2, slots)), dma((2, slots)), dma((slots,)), dma((slots,)),
            dma((slots,)), dma((2, slots)), dma((2, slots)), dma((2,)), dma((3,)),
        ],
        compiler_params=pltpu.CompilerParams(
            collective_id=0, has_side_effects=True, vmem_limit_bytes=62 * 1024 * 1024
        ),
        name="exchange",
    )(g_less.reshape(shape), g_greater.reshape(shape), coulomb[0], forward, inverse)


def gather_kernel(picks, below, own, above, out_ref):
    slot = pl.program_id(0)
    total = own[0].astype(jnp.float32)
    total += jnp.where(picks[2, slot] > 0, below[0].astype(jnp.float32), 0.0)
    total += jnp.where(picks[3, slot] > 0, above[0].astype(jnp.float32), 0.0)
    out_ref[:, :, 0] = total.astype(jnp.bfloat16)


def shards(g_less, g_greater, coulomb, pattern):
    e_local, rows_local, slots, orbitals, cols = g_less.shape
    own, below, above = polarization(g_less, g_greater, coulomb)
    _, local, radix, _, _ = own.shape
    start_row = lax.axis_index("slab")
    filler = jnp.full((1, slots), -1, jnp.int32)
    extended = jnp.concatenate([filler, pattern, filler], 0)
    near = lax.dynamic_slice_in_dim(extended, start_row, 3, 0)
    match = near[::2, None, :] == near[1][None, :, None]
    slot_index = jnp.arange(slots, dtype=jnp.int32)
    place = jnp.sum(jnp.where(match, slot_index, 0), -1)
    found = jnp.sum(match.astype(jnp.int32), -1)
    picks = jnp.concatenate([place, found], 0)

    def side(d):
        return pl.BlockSpec(
            (1, local, radix, orbitals, cols), lambda s, picks: (picks[d, s], 0, 0, 0, 0)
        )

    out = pl.pallas_call(
        gather_kernel,
        out_shape=jax.ShapeDtypeStruct((local, radix, slots, orbitals, cols), jnp.bfloat16),
        grid_spec=pltpu.PrefetchScalarGridSpec(
            num_scalar_prefetch=1,
            grid=(slots,),
            in_specs=[
                side(0),
                pl.BlockSpec((1, local, radix, orbitals, cols), lambda s, picks: (s, 0, 0, 0, 0)),
                side(1),
            ],
            out_specs=pl.BlockSpec(
                (local, radix, 1, orbitals, cols), lambda s, picks: (0, 0, s, 0, 0)
            ),
        ),
        name="gather",
    )(picks, below, own, above)
    return out.reshape(e_local, rows_local, slots, orbitals, cols)


def solution(mesh):
    placed = (
        P("energy", "slab", None, None, None),
        P("energy", "slab", None, None, None),
        P("slab", None, None),
        P(),
    )
    return jax.shard_map(
        shards,
        mesh=mesh,
        in_specs=placed,
        out_specs=P("energy", "slab", None, None, None),
        check_vma=False,
    )
```

profile of v0, /device:TPU:0, one launch (start us, length us, event | category | flops | bytes accessed | tf_op | source)
XLA Modules:
  0.0 362.4 jit_solution(12224968136685060704)
XLA Ops:
  0.0 0.7 pad_add_fusion
  0.7 0.3 fusion
  1.1 0.1 copy.8
  1.1 0.1 copy.9
  1.2 0.6 pad_add_fusion.1.picks
  1.8 351.5 %exchange.1 = (bf16[5,16,4,64,128]{4,3,2,1,0:T(8,128)(2,1)}, bf16[5,16,4,64,128]{4,3,2,1,0:T(8,128)(2,1)}, bf16[5,16,4,64,128]{4,3,2,1,0:T(8,128)(2,1)}) custom-call(bf16[16,4,5,64,128]{4,3,2,1,0:T(8,128)(2,1)} %bitcast.8, bf16[16,4,5,64,128]{4,3,2,1,0:T(8,128)(2,1)} %bitcast.9, bf16[64,192]{1,0:T(8,128)(2,1)} %bitcast.10, ...), custom_call_target="tpu_custom_call" | custom-call | tf_op jit(solution)/shard_map/exchange/pallas_call | solution.py:321
  353.3 9.1 %gather.1 = bf16[16,4,5,64,128]{4,3,2,1,0:T(8,128)(2,1)} custom-call(s32[4,5]{1,0:T(4,128)} %pad_add_fusion.1.picks, bf16[5,16,4,64,128]{4,3,2,1,0:T(8,128)(2,1)} %get-tuple-element.8.below, bf16[5,16,4,64,128]{4,3,2,1,0:T(8,128)(2,1)} %get-tuple-element.9.own, bf16[5,16,4,64,128]{4,3,2,1,0:T(8,128)(2,1)} %get-tuple-element.10.above), custom_call_target="tpu_custom_call" | custom-call | tf_op jit(solution)/shard_map/gather/pallas_call | solution.py:372
  (4 shorter events, 0.0 us)
where the time goes:
time: 363 us; the launch traced here: 362 us
  Pallas kernels  361 us (99%)
    pallas_call x1, Pallas kernels, polarization(): pl.pallas_call(functools.partial(exchange_kernel, peers, rows, radix), ou...  351 us
    pallas_call x1, Pallas kernels, shards(): pl.pallas_call(gather_kernel, out_shape=jax.ShapeDtypeStruct((local, radi...  9.15 us

commit v1 on v0

v1 whole, which is shorter than its diff:
```python
import functools
import math

import jax
import jax.numpy as jnp
import numpy as np
from jax import lax
from jax.experimental import pallas as pl
from jax.experimental.pallas import tpu as pltpu
from jax.sharding import PartitionSpec as P

MESH = pl.DeviceIdType.MESH
LANES = 128
TILE = 16


def make_tables(count):
    index = np.arange(count)
    angles = (index[:, None] * index[None, :] % count) * (2.0 * math.pi / count)
    scale = 1.0 / math.sqrt(count)
    table_real = (np.cos(angles) * scale).astype(np.float32).astype(jnp.bfloat16)
    table_imag = (-np.sin(angles) * scale).astype(np.float32).astype(jnp.bfloat16)
    return table_real, table_imag


def split_tables(count, radix):
    part = count // radix
    cut = np.stack(make_tables(count))[:, :part, :].reshape(2, part, part, radix)
    return np.ascontiguousarray(cut.transpose(0, 3, 1, 2)), np.ascontiguousarray(cut.transpose(0, 3, 2, 1))


def turn(values, sign):
    return sign * pltpu.roll(values, LANES // 2, 1)


def guarded(there, action):
    if there is None:
        action()
    else:
        pl.when(there)(action)


def exchange_kernel(
    peers, count, radix, less_hbm, great_hbm, coulomb_hbm, pattern_hbm, fwd_hbm, inv_hbm, out_ref,
    stage, send, held, reply, back, own, near, fwd_ref, inv_ref, coulomb_ref, pattern_ref, weights,
    load_sem, side_sem, send_sem, recv_sem, back_send, back_recv, near_send, near_recv,
):
    me = lax.axis_index("energy")
    row = lax.axis_index("slab")
    slots = send.shape[1]
    local = send.shape[4]
    wide = send.shape[5]
    quads = wide // LANES
    orbitals = stage.shape[3]
    sides = min(count - 1, 2)
    has_below, has_above = row > 0, row < count - 1

    if count == 2:
        origins = ((None, 1 - row, 2 - 2 * row),)
        links = ((None, 1 - row, 0),)
    elif count > 2:
        origins = (
            (has_below, lax.rem(row + count - 1, count), 0),
            (has_above, lax.rem(row + 1, count), 2),
        )
        links = ((has_above, row + 1, 0), (has_below, row - 1, 1))
    else:
        origins, links = (), ()

    barrier = pltpu.get_barrier_semaphore()
    half = peers // 2

    def partner(step):
        if peers & (peers - 1):
            return lax.rem(me + step + 1, peers)
        odd = lax.rem(step, 2)
        mask = (1 - odd) * half + lax.div(step + odd, 2)
        peer, bit = 0, 1
        while bit < peers:
            peer = peer + bit * lax.rem(lax.div(me, bit) + lax.div(mask, bit), 2)
            bit *= 2
        return peer

    def greet(step, carry):
        pl.semaphore_signal(
            barrier, inc=1, device_id={"energy": partner(step)}, device_id_type=MESH
        )
        return carry

    def load(which, slot, buf):
        source = (less_hbm, great_hbm)[which]
        return pltpu.make_async_copy(source.at[:, :, slot], stage.at[buf], load_sem.at[buf])

    lax.fori_loop(0, peers - 1, greet, 0)
    greeted = peers - 1
    for there, peer, _ in links:
        def meet(peer=peer):
            pl.semaphore_signal(barrier, inc=1, device_id={"slab": peer}, device_id_type=MESH)

        guarded(there, meet)
        greeted = greeted + (1 if there is None else there.astype(jnp.int32))

    load(0, 0, 0).start()
    fetches = [
        pltpu.make_async_copy(source, target, side_sem.at[k])
        for k, (source, target) in enumerate(
            (
                (fwd_hbm, fwd_ref), (inv_hbm, inv_ref),
                (coulomb_hbm, coulomb_ref), (pattern_hbm, pattern_ref),
            )
        )
    ]

    lane = lax.broadcasted_iota(jnp.int32, (1, LANES), 1)
    sign = jnp.where(lane < LANES // 2, -1.0, 1.0).astype(jnp.float32)
    mine = pl.ds(pl.multiple_of(me * local, local), local)

    def scatter(which, slot):
        load(which, slot, which).wait()
        if which == 0:
            load(1, slot, 1).start()
        else:
            @pl.when(slot + 1 < slots)
            def _():
                load(0, slot + 1, 0).start()

        def cut(group, carry):
            top = pl.multiple_of(group * TILE, TILE)
            for r in range(radix):
                tile = stage[which, :, r, pl.ds(top, TILE), :].astype(jnp.float32)
                tile = jnp.swapaxes(tile, 0, 1).astype(jnp.bfloat16)
                for k in range(TILE):
                    send[which, slot, group * (TILE // quads) + k // quads, r, :,
                         (k % quads) * LANES : (k % quads + 1) * LANES] = tile[k]
            return carry

        lax.fori_loop(0, orbitals // TILE, cut, 0)
        if which == 0:
            @pl.when(slot == 0)
            def _():
                for fetch in fetches:
                    fetch.start()
                pl.semaphore_wait(barrier, greeted)

        def ship(step, carry):
            peer = partner(step)
            pltpu.make_async_remote_copy(
                src_ref=send.at[which, slot, peer],
                dst_ref=held.at[which, slot, :, mine, :],
                send_sem=send_sem.at[which, slot],
                recv_sem=recv_sem.at[which, slot],
                device_id={"energy": peer},
                device_id_type=MESH,
            ).start()
            return carry

        lax.fori_loop(0, peers - 1, ship, 0)
        pltpu.make_async_copy(
            send.at[which, slot, me], held.at[which, slot, :, mine, :], recv_sem.at[which, slot]
        ).start()

    def scatter_slot(slot, carry):
        scatter(0, slot)
        scatter(1, slot)
        return carry

    lax.fori_loop(0, slots, scatter_slot, 0)
    for fetch in fetches:
        fetch.wait()

    span = orbitals * (1 + sides)
    depth = slots * span
    entry = lax.broadcasted_iota(jnp.int32, (3 * orbitals, depth), 0)
    place = lax.broadcasted_iota(jnp.int32, (1, depth), 1)
    block = place // orbitals
    inner = lax.rem(place, orbitals)
    column = jnp.full((1, depth), -1, jnp.int32)
    piece = jnp.full((1, depth), 1, jnp.int32)
    for t in range(slots):
        at = t * (1 + sides)
        column = jnp.where(block == at, pattern_ref[row, t], column)
        for side, (there, k, d) in enumerate(origins):
            there = 1 if there is None else there.astype(jnp.int32)
            seen = there * (pattern_ref[k, t] + 1) - 1
            column = jnp.where(block == at + 1 + side, seen, column)
            piece = jnp.where(block == at + 1 + side, d, piece)
    wanted = lax.rem(inner, peers) * quads + inner // peers + piece * orbitals
    for s in range(slots):
        goal = jnp.where(column == pattern_ref[row, s], wanted, -1)
        select = (entry == goal).astype(jnp.float32).astype(jnp.bfloat16)
        part_of = jnp.dot(coulomb_ref[...], select, preferred_element_type=jnp.float32)
        weights[s * orbitals : (s + 1) * orbitals, :] = part_of.astype(jnp.bfloat16)

    for side, (there, _, _) in enumerate(origins):
        if there is not None:
            @pl.when(jnp.logical_not(there))
            def _(side=side):
                near[side] = jnp.zeros(near.shape[1:], near.dtype)

    def forward(which, slot, col):
        pieces = []
        for r in range(radix):
            block = held[which, slot, r, :, col]
            direct = jnp.dot(fwd_ref[0, r], block, preferred_element_type=jnp.float32)
            crossed = jnp.dot(fwd_ref[1, r], block, preferred_element_type=jnp.float32)
            pieces.append(direct + turn(crossed, sign))
        if radix == 1:
            return pieces
        even, odd = pieces[0] + pieces[2], pieces[1] + pieces[3]
        gap, twist = pieces[0] - pieces[2], turn(pieces[1] - pieces[3], sign)
        return [even + odd, gap - twist, even - odd, gap + twist]

    def compute(slot, carry):
        for which in range(2):
            pltpu.make_async_copy(
                held.at[which, slot], held.at[which, slot], recv_sem.at[which, slot]
            ).wait()
        for quad in range(quads):
            col = slice(quad * LANES, (quad + 1) * LANES)
            lesser = forward(0, slot, col)
            greater = forward(1, slot, col)
            products = []
            for a, b in zip(lesser, greater):
                along = a * b
                across = a * pltpu.roll(b, LANES // 2, 1)
                products.append(
                    jnp.where(
                        lane < LANES // 2,
                        along + pltpu.roll(along, LANES // 2, 1),
                        across - pltpu.roll(across, LANES // 2, 1),
                    )
                )
            if radix == 4:
                z0, z1, z2, z3 = products
                even, odd = z0 + z2, z1 + z3
                gap, twist = z0 - z2, turn(z1 - z3, sign)
                products = [even + odd, gap + twist, even - odd, gap - twist]
            for r in range(radix):
                block = products[r].astype(jnp.bfloat16)
                direct = jnp.dot(inv_ref[0, r], block, preferred_element_type=jnp.float32)
                crossed = jnp.dot(inv_ref[1, r], block, preferred_element_type=jnp.float32)
                reply[slot, r, :, col] = (direct - turn(crossed, sign)).astype(jnp.bfloat16)

        for r in range(radix):
            def ship(step, carry, r=r):
                peer = partner(step)
                rows = pl.ds(pl.multiple_of(peer * local, local), local)
                pltpu.make_async_remote_copy(
                    src_ref=reply.at[slot, r, rows, :],
                    dst_ref=back.at[slot, r, me],
                    send_sem=back_send.at[slot],
                    recv_sem=back_recv.at[slot, r],
                    device_id={"energy": peer},
                    device_id_type=MESH,
                ).start()
                return carry

            lax.fori_loop(0, peers - 1, ship, 0)
            pltpu.make_async_copy(
                reply.at[slot, r, mine, :], back.at[slot, r, me], back_recv.at[slot, r]
            ).start()
        return carry

    lax.fori_loop(0, slots, compute, 0)

    def hand(link, slot, r):
        _, peer, side = links[link]
        return pltpu.make_async_remote_copy(
            src_ref=own.at[slot, r],
            dst_ref=near.at[side, slot, r],
            send_sem=near_send.at[link, slot, r],
            recv_sem=near_recv.at[side, slot, r],
            device_id={"slab": peer},
            device_id_type=MESH,
        )

    def collect(slot, r):
        pltpu.make_async_copy(back.at[slot, r], back.at[slot, r], back_recv.at[slot, r]).wait()
        for quad in range(quads):
            tile = back[slot, r, :, :, quad * LANES : (quad + 1) * LANES]
            tile = jnp.swapaxes(tile.astype(jnp.float32), 0, 1).astype(jnp.bfloat16)
            own[slot, r, :, quad * peers : (quad + 1) * peers, :] = tile
        for link, (there, _, _) in enumerate(links):
            guarded(there, lambda link=link: hand(link, slot, r).start())

    def screen(r):
        for side, (there, _, _) in enumerate(origins):
            def arrived(side=side):
                for slot in range(slots):
                    block = near.at[side, slot, r]
                    pltpu.make_async_copy(block, block, near_recv.at[side, slot, r]).wait()

            guarded(there, arrived)

        def pair(k, carry):
            columns = []
            for e in (2 * k, 2 * k + 1):
                rows = []
                for slot in range(slots):
                    rows.append(own[slot, r, e])
                    for side in range(sides):
                        rows.append(near[side, slot, r, e])
                columns.append(jnp.concatenate(rows, 0))
            both = jnp.dot(
                weights[...], jnp.concatenate(columns, 1), preferred_element_type=jnp.float32
            ).astype(jnp.bfloat16)
            for j in range(2):
                for slot in range(slots):
                    out_ref[(2 * k + j) * radix + r, 0, slot] = both[
                        slot * orbitals : (slot + 1) * orbitals, j * LANES : (j + 1) * LANES
                    ]
            return carry

        lax.fori_loop(0, local // 2, pair, 0)

    def collect_slot(slot, carry):
        for r in range(radix):
            collect(slot, r)
        return carry

    lax.fori_loop(0, slots - 1, collect_slot, 0)
    for r in range(radix):
        collect(slots - 1, r)
        if r > 0:
            screen(r - 1)
    screen(radix - 1)

    def finish(slot, carry):
        rest = pl.ds(0, peers - 1)
        for which in range(2):
            pltpu.make_async_copy(
                send.at[which, slot, rest], send.at[which, slot, rest], send_sem.at[which, slot]
            ).wait()
        pltpu.make_async_copy(
            send.at[0, slot, rest], send.at[0, slot, rest], back_send.at[slot]
        ).wait()
        for link, (there, _, _) in enumerate(links):
            def gone(link=link):
                for r in range(radix):
                    hand(link, slot, r).wait_send()

            guarded(there, gone)
        return carry

    lax.fori_loop(0, slots, finish, 0)


def shards(g_less, g_greater, coulomb, pattern):
    e_local, _, slots, orbitals, cols = g_less.shape
    peers, rows = lax.axis_size("energy"), lax.axis_size("slab")
    count = e_local * peers
    radix = 4 if e_local % 64 == 0 else 1
    part = count // radix
    local = e_local // radix
    wide = orbitals // peers * cols
    sides = min(rows - 1, 2)
    forward, inverse = split_tables(count, radix)
    shape = (local, radix, slots, orbitals, cols)
    hbm = pl.BlockSpec(memory_space=pltpu.HBM)
    bf16 = jnp.bfloat16
    dma = pltpu.SemaphoreType.DMA
    operands = (g_less.reshape(shape), g_greater.reshape(shape), coulomb[0], pattern, forward, inverse)
    pin = lambda array: pltpu.with_memory_space_constraint(array, pltpu.HBM)
    out = pl.pallas_call(
        functools.partial(exchange_kernel, peers, rows, radix),
        out_shape=jax.ShapeDtypeStruct(g_less.shape, bf16),
        in_specs=[hbm] * 6,
        out_specs=pl.BlockSpec(memory_space=pltpu.VMEM),
        scratch_shapes=[
            pltpu.VMEM((2, local, radix, orbitals, cols), bf16),
            pltpu.VMEM((2, slots, peers, radix, local, wide), bf16),
            pltpu.VMEM((2, slots, radix, part, wide), bf16),
            pltpu.VMEM((slots, radix, part, wide), bf16),
            pltpu.VMEM((slots, radix, peers, local, wide), bf16),
            pltpu.VMEM((slots, radix, local, orbitals, cols), bf16),
            pltpu.VMEM((max(sides, 1), slots, radix, local, orbitals, cols), bf16),
            pltpu.VMEM(forward.shape, bf16),
            pltpu.VMEM(inverse.shape, bf16),
            pltpu.VMEM(coulomb.shape[1:], bf16),
            pltpu.SMEM(pattern.shape, jnp.int32),
            pltpu.VMEM((slots * orbitals, slots * orbitals * (1 + sides)), bf16),
            dma((2,)), dma((4,)), dma((2, slots)), dma((2, slots)), dma((slots,)),
            dma((slots, radix)), dma((max(sides, 1), slots, radix)),
            dma((max(sides, 1), slots, radix)),
        ],
        compiler_params=pltpu.CompilerParams(
            collective_id=0, has_side_effects=True, vmem_limit_bytes=47 * 1024 * 1024
        ),
        name="exchange",
    )(*map(pin, operands))
    return out


def solution(mesh):
    placed = (
        P("energy", "slab", None, None, None),
        P("energy", "slab", None, None, None),
        P("slab", None, None),
        P(),
    )
    return jax.shard_map(
        shards,
        mesh=mesh,
        in_specs=placed,
        out_specs=P("energy", "slab", None, None, None),
        check_vma=False,
    )
```

time: 363 us -> 354 us (0.975)
  Pallas kernels: 361 us -> 351 us
    pallas_call x2 -> x1, Pallas kernels: 361 us -> 351 us  [shards(): pl.pallas_call(functools.partial(exchange_kernel, peers, rows, radix), ou...]
where the time goes in v1:
time: 354 us; the launch traced here: 353 us
  Pallas kernels  351 us (99%)
    pallas_call x1, Pallas kernels, shards(): pl.pallas_call(functools.partial(exchange_kernel, peers, rows, radix), ou...  351 us

profile of v1, /device:TPU:0, one launch (start us, length us, event | category | flops | bytes accessed | tf_op | source)
XLA Modules:
  0.0 353.2 jit_solution(12964471977444676912)
XLA Ops:
  0.0 350.8 %exchange.1 = bf16[64,1,5,64,128]{4,3,2,1,0:T(8,128)(2,1)S(1)} custom-call(bf16[16,4,5,64,128]{4,3,2,1,0:T(8,128)(2,1)} %bitcast.3, bf16[16,4,5,64,128]{4,3,2,1,0:T(8,128)(2,1)} %bitcast.4, bf16[64,192]{1,0:T(8,128)(2,1)} %bitcast.5, s32[2,5]{1,0:T(2,128)} %pattern_hbm.1, bf16[2,4,256,256]{3,2,1,0:T(8,128)(2,1)} %constant.4.clone.fwd_hbm, ...), custom_call_target="tpu_custom_call" | custom-call | tf_op jit(solution)/shard_map/exchange/pallas_call | solution.py:364
  350.8 2.4 copy.8

commit v2 on v1

--- a/solution.py
+++ b/solution.py
@@ -147,7 +147,7 @@
             pltpu.make_async_remote_copy(
                 src_ref=send.at[which, slot, peer],
                 dst_ref=held.at[which, slot, :, mine, :],
-                send_sem=send_sem.at[which, slot],
+                send_sem=send_sem.at[which],
                 recv_sem=recv_sem.at[which, slot],
                 device_id={"energy": peer},
                 device_id_type=MESH,
@@ -248,7 +248,7 @@
                 pltpu.make_async_remote_copy(
                     src_ref=reply.at[slot, r, rows, :],
                     dst_ref=back.at[slot, r, me],
-                    send_sem=back_send.at[slot],
+                    send_sem=back_send.at[0],
                     recv_sem=back_recv.at[slot, r],
                     device_id={"energy": peer},
                     device_id_type=MESH,
@@ -268,8 +268,8 @@
         return pltpu.make_async_remote_copy(
             src_ref=own.at[slot, r],
             dst_ref=near.at[side, slot, r],
-            send_sem=near_send.at[link, slot, r],
-            recv_sem=near_recv.at[side, slot, r],
+            send_sem=near_send.at[link],
+            recv_sem=near_recv.at[side, r],
             device_id={"slab": peer},
             device_id_type=MESH,
         )
@@ -286,15 +286,14 @@
     def screen(r):
         for side, (there, _, _) in enumerate(origins):
             def arrived(side=side):
-                for slot in range(slots):
-                    block = near.at[side, slot, r]
-                    pltpu.make_async_copy(block, block, near_recv.at[side, slot, r]).wait()
+                block = near.at[side, :, r]
+                pltpu.make_async_copy(block, block, near_recv.at[side, r]).wait()
 
             guarded(there, arrived)
 
-        def pair(k, carry):
+        for first in range(0, local, 2):
             columns = []
-            for e in (2 * k, 2 * k + 1):
+            for e in (first, first + 1):
                 rows = []
                 for slot in range(slots):
                     rows.append(own[slot, r, e])
@@ -306,12 +305,9 @@
             ).astype(jnp.bfloat16)
             for j in range(2):
                 for slot in range(slots):
-                    out_ref[(2 * k + j) * radix + r, 0, slot] = both[
+                    out_ref[(first + j) * radix + r, 0, slot] = both[
                         slot * orbitals : (slot + 1) * orbitals, j * LANES : (j + 1) * LANES
                     ]
-            return carry
-
-        lax.fori_loop(0, local // 2, pair, 0)
 
     def collect_slot(slot, carry):
         for r in range(radix):
@@ -319,30 +315,19 @@
         return carry
 
     lax.fori_loop(0, slots - 1, collect_slot, 0)
+    rest = pl.ds(0, peers - 1)
+    for which in range(2):
+        pltpu.make_async_copy(
+            send.at[which, :, rest], send.at[which, :, rest], send_sem.at[which]
+        ).wait()
     for r in range(radix):
         collect(slots - 1, r)
         if r > 0:
             screen(r - 1)
     screen(radix - 1)
-
-    def finish(slot, carry):
-        rest = pl.ds(0, peers - 1)
-        for which in range(2):
-            pltpu.make_async_copy(
-                send.at[which, slot, rest], send.at[which, slot, rest], send_sem.at[which, slot]
-            ).wait()
-        pltpu.make_async_copy(
-            send.at[0, slot, rest], send.at[0, slot, rest], back_send.at[slot]
-        ).wait()
-        for link, (there, _, _) in enumerate(links):
-            def gone(link=link):
-                for r in range(radix):
-                    hand(link, slot, r).wait_send()
-
-            guarded(there, gone)
-        return carry
-
-    lax.fori_loop(0, slots, finish, 0)
+    pltpu.make_async_copy(send.at[0, :, rest], send.at[0, :, rest], back_send.at[0]).wait()
+    for link, (there, _, _) in enumerate(links):
+        guarded(there, pltpu.make_async_copy(own, own, near_send.at[link]).wait)
 
 
 def shards(g_less, g_greater, coulomb, pattern):
@@ -379,9 +364,8 @@
             pltpu.VMEM(coulomb.shape[1:], bf16),
             pltpu.SMEM(pattern.shape, jnp.int32),
             pltpu.VMEM((slots * orbitals, slots * orbitals * (1 + sides)), bf16),
-            dma((2,)), dma((4,)), dma((2, slots)), dma((2, slots)), dma((slots,)),
-            dma((slots, radix)), dma((max(sides, 1), slots, radix)),
-            dma((max(sides, 1), slots, radix)),
+            dma((2,)), dma((4,)), dma((2,)), dma((2, slots)), dma((1,)), dma((slots, radix)),
+            dma((max(sides, 1),)), dma((max(sides, 1), radix)),
         ],
         compiler_params=pltpu.CompilerParams(
             collective_id=0, has_side_effects=True, vmem_limit_bytes=47 * 1024 * 1024

time: 354 us -> 351 us (level)
  no operation moved by 1% of the time
where the time goes in v2:
time: 351 us; the launch traced here: 350 us
  Pallas kernels  348 us (99%)
    pallas_call x1, Pallas kernels, shards(): pl.pallas_call(functools.partial(exchange_kernel, peers, rows, radix), ou...  348 us

profile of v2, /device:TPU:0, one launch (start us, length us, event | category | flops | bytes accessed | tf_op | source)
XLA Modules:
  0.0 350.3 jit_solution(14186801615560256939)
XLA Ops:
  0.0 348.0 %exchange.1 = bf16[64,1,5,64,128]{4,3,2,1,0:T(8,128)(2,1)S(1)} custom-call(bf16[16,4,5,64,128]{4,3,2,1,0:T(8,128)(2,1)} %bitcast.3, bf16[16,4,5,64,128]{4,3,2,1,0:T(8,128)(2,1)} %bitcast.4, bf16[64,192]{1,0:T(8,128)(2,1)} %bitcast.5, s32[2,5]{1,0:T(2,128)} %pattern_hbm.1, bf16[2,4,256,256]{3,2,1,0:T(8,128)(2,1)} %constant.4.clone.fwd_hbm, ...), custom_call_target="tpu_custom_call" | custom-call | tf_op jit(solution)/shard_map/exchange/pallas_call | solution.py:349
  348.0 2.4 copy.8

commit v3 on v2

--- a/solution.py
+++ b/solution.py
@@ -41,8 +41,9 @@
 
 
 def exchange_kernel(
-    peers, count, radix, less_hbm, great_hbm, coulomb_hbm, pattern_hbm, fwd_hbm, inv_hbm, out_ref,
-    stage, send, held, reply, back, own, near, fwd_ref, inv_ref, coulomb_ref, pattern_ref, weights,
+    peers, count, radix, less_hbm, great_hbm, coulomb_hbm, pattern_hbm, fwd_hbm, inv_hbm,
+    done, own_last, near_last, weights,
+    stage, send, held, reply, back, own, near, fwd_ref, inv_ref, coulomb_ref, pattern_ref,
     load_sem, side_sem, send_sem, recv_sem, back_send, back_recv, near_send, near_recv,
 ):
     me = lax.axis_index("energy")
@@ -196,6 +197,7 @@
             @pl.when(jnp.logical_not(there))
             def _(side=side):
                 near[side] = jnp.zeros(near.shape[1:], near.dtype)
+                near_last[side] = jnp.zeros(near_last.shape[1:], near_last.dtype)
 
     def forward(which, slot, col):
         pieces = []
@@ -263,12 +265,14 @@
 
     lax.fori_loop(0, slots, compute, 0)
 
+    last = radix - 1
+
     def hand(link, slot, r):
         _, peer, side = links[link]
         return pltpu.make_async_remote_copy(
-            src_ref=own.at[slot, r],
-            dst_ref=near.at[side, slot, r],
-            send_sem=near_send.at[link],
+            src_ref=own_last.at[slot] if r == last else own.at[slot, r],
+            dst_ref=near_last.at[side, slot] if r == last else near.at[side, slot, r],
+            send_sem=near_send.at[link, r],
             recv_sem=near_recv.at[side, r],
             device_id={"slab": peer},
             device_id_type=MESH,
@@ -276,38 +280,37 @@
 
     def collect(slot, r):
         pltpu.make_async_copy(back.at[slot, r], back.at[slot, r], back_recv.at[slot, r]).wait()
+        target = own_last.at[slot] if r == last else own.at[slot, r]
         for quad in range(quads):
             tile = back[slot, r, :, :, quad * LANES : (quad + 1) * LANES]
             tile = jnp.swapaxes(tile.astype(jnp.float32), 0, 1).astype(jnp.bfloat16)
-            own[slot, r, :, quad * peers : (quad + 1) * peers, :] = tile
+            target[:, quad * peers : (quad + 1) * peers, :] = tile
         for link, (there, _, _) in enumerate(links):
             guarded(there, lambda link=link: hand(link, slot, r).start())
 
+    def arrived(r):
+        for side, (there, _, _) in enumerate(origins):
+            block = near_last.at[side] if r == last else near.at[side, :, r]
+            guarded(there, pltpu.make_async_copy(block, block, near_recv.at[side, r]).wait)
+
+    def handed(r):
+        for link, (there, _, _) in enumerate(links):
+            guarded(there, pltpu.make_async_copy(own_last, own_last, near_send.at[link, r]).wait)
+
     def screen(r):
-        for side, (there, _, _) in enumerate(origins):
-            def arrived(side=side):
-                block = near.at[side, :, r]
-                pltpu.make_async_copy(block, block, near_recv.at[side, r]).wait()
-
-            guarded(there, arrived)
-
+        arrived(r)
+        handed(r)
         for first in range(0, local, 2):
-            columns = []
+            pairs = []
             for e in (first, first + 1):
                 rows = []
                 for slot in range(slots):
                     rows.append(own[slot, r, e])
-                    for side in range(sides):
-                        rows.append(near[side, slot, r, e])
-                columns.append(jnp.concatenate(rows, 0))
-            both = jnp.dot(
-                weights[...], jnp.concatenate(columns, 1), preferred_element_type=jnp.float32
-            ).astype(jnp.bfloat16)
-            for j in range(2):
+                    rows.extend(near[side, slot, r, e] for side in range(sides))
+                pairs.append(jnp.concatenate(rows, 0))
+            for j, block in enumerate(products(weights, pairs)):
                 for slot in range(slots):
-                    out_ref[(first + j) * radix + r, 0, slot] = both[
-                        slot * orbitals : (slot + 1) * orbitals, j * LANES : (j + 1) * LANES
-                    ]
+                    done[r, first + j, slot] = block[slot * orbitals : (slot + 1) * orbitals]
 
     def collect_slot(slot, carry):
         for r in range(radix):
@@ -324,10 +327,52 @@
         collect(slots - 1, r)
         if r > 0:
             screen(r - 1)
-    screen(radix - 1)
     pltpu.make_async_copy(send.at[0, :, rest], send.at[0, :, rest], back_send.at[0]).wait()
-    for link, (there, _, _) in enumerate(links):
-        guarded(there, pltpu.make_async_copy(own, own, near_send.at[link]).wait)
+    arrived(last)
+    handed(last)
+
+
+def products(weights, pairs):
+    both = jnp.dot(weights[...], jnp.concatenate(pairs, 1), preferred_element_type=jnp.float32)
+    both = both.astype(jnp.bfloat16)
+    return [both[:, j * LANES : (j + 1) * LANES] for j in range(len(pairs))]
+
+
+def finish_kernel(done, own_ref, near_ref, weights, out_hbm, tail, copy_sem, tail_sem):
+    slots, local, orbitals, _ = own_ref.shape
+    sides = near_ref.shape[0] if weights.shape[1] > slots * orbitals else 0
+    last = out_hbm.shape[1] - 1
+    share = local // 2
+    copies = [
+        pltpu.make_async_copy(
+            done.at[r, pl.ds(half * share, share)],
+            out_hbm.at[pl.ds(half * share, share), r],
+            copy_sem.at[r, half],
+        )
+        for r in range(last)
+        for half in range(2)
+    ]
+    for copy in copies:
+        copy.start()
+    for half in range(2):
+        for first in range(half * share, (half + 1) * share, 2):
+            pairs = []
+            for e in (first, first + 1):
+                rows = []
+                for slot in range(slots):
+                    rows.append(own_ref[slot, e])
+                    rows.extend(near_ref[side, slot, e] for side in range(sides))
+                pairs.append(jnp.concatenate(rows, 0))
+            for j, block in enumerate(products(weights, pairs)):
+                for slot in range(slots):
+                    tail[first + j, slot] = block[slot * orbitals : (slot + 1) * orbitals]
+        some = pl.ds(half * share, share)
+        copies.append(
+            pltpu.make_async_copy(tail.at[some], out_hbm.at[some, last], tail_sem.at[half])
+        )
+        copies[-1].start()
+    for copy in copies:
+        copy.wait()
 
 
 def shards(g_less, g_greater, coulomb, pattern):
@@ -346,33 +391,50 @@
     dma = pltpu.SemaphoreType.DMA
     operands = (g_less.reshape(shape), g_greater.reshape(shape), coulomb[0], pattern, forward, inverse)
     pin = lambda array: pltpu.with_memory_space_constraint(array, pltpu.HBM)
-    out = pl.pallas_call(
+    kept = max(radix - 1, 1)
+    vmem = pl.BlockSpec(memory_space=pltpu.VMEM)
+    done, own, near, weights = pl.pallas_call(
         functools.partial(exchange_kernel, peers, rows, radix),
-        out_shape=jax.ShapeDtypeStruct(g_less.shape, bf16),
+        out_shape=[
+            jax.ShapeDtypeStruct((kept, local, slots, orbitals, cols), bf16),
+            jax.ShapeDtypeStruct((slots, local, orbitals, cols), bf16),
+            jax.ShapeDtypeStruct((max(sides, 1), slots, local, orbitals, cols), bf16),
+            jax.ShapeDtypeStruct((slots * orbitals, slots * orbitals * (1 + sides)), bf16),
+        ],
         in_specs=[hbm] * 6,
-        out_specs=pl.BlockSpec(memory_space=pltpu.VMEM),
+        out_specs=[vmem] * 4,
         scratch_shapes=[
             pltpu.VMEM((2, local, radix, orbitals, cols), bf16),
             pltpu.VMEM((2, slots, peers, radix, local, wide), bf16),
             pltpu.VMEM((2, slots, radix, part, wide), bf16),
             pltpu.VMEM((slots, radix, part, wide), bf16),
             pltpu.VMEM((slots, radix, peers, local, wide), bf16),
-            pltpu.VMEM((slots, radix, local, orbitals, cols), bf16),
-            pltpu.VMEM((max(sides, 1), slots, radix, local, orbitals, cols), bf16),
+            pltpu.VMEM((slots, kept, local, orbitals, cols), bf16),
+            pltpu.VMEM((max(sides, 1), slots, kept, local, orbitals, cols), bf16),
             pltpu.VMEM(forward.shape, bf16),
             pltpu.VMEM(inverse.shape, bf16),
             pltpu.VMEM(coulomb.shape[1:], bf16),
             pltpu.SMEM(pattern.shape, jnp.int32),
-            pltpu.VMEM((slots * orbitals, slots * orbitals * (1 + sides)), bf16),
             dma((2,)), dma((4,)), dma((2,)), dma((2, slots)), dma((1,)), dma((slots, radix)),
-            dma((max(sides, 1),)), dma((max(sides, 1), radix)),
+            dma((max(sides, 1), radix)), dma((max(sides, 1), radix)),
         ],
         compiler_params=pltpu.CompilerParams(
-            collective_id=0, has_side_effects=True, vmem_limit_bytes=47 * 1024 * 1024
+            collective_id=0, has_side_effects=True, vmem_limit_bytes=44 * 1024 * 1024
         ),
         name="exchange",
     )(*map(pin, operands))
-    return out
+    out = pl.pallas_call(
+        finish_kernel,
+        out_shape=jax.ShapeDtypeStruct(shape, bf16),
+        in_specs=[pl.BlockSpec(memory_space=pl.ANY), vmem, vmem, vmem],
+        out_specs=pl.BlockSpec(memory_space=pltpu.HBM),
+        scratch_shapes=[
+            pltpu.VMEM((local, slots, orbitals, cols), bf16), dma((kept, 2)), dma((2,)),
+        ],
+        compiler_params=pltpu.CompilerParams(vmem_limit_bytes=16 * 1024 * 1024),
+        name="finish",
+    )(done, own, near, weights)
+    return out.reshape(g_less.shape)
 
 
 def solution(mesh):

time: 351 us -> 350 us (level)
  no operation moved by 1% of the time
where the time goes in v3:
time: 350 us; the launch traced here: 349 us
  Pallas kernels  349 us (100%)
    pallas_call x1, Pallas kernels, shards(): pl.pallas_call(functools.partial(exchange_kernel, peers, rows, radix), ou...  347 us

profile of v3, /device:TPU:0, one launch (start us, length us, event | category | flops | bytes accessed | tf_op | source)
XLA Modules:
  0.0 349.3 jit_solution(2856003959597616738)
XLA Ops:
  0.0 346.8 %exchange.1 = (bf16[3,16,5,64,128]{4,3,2,1,0:T(8,128)(2,1)S(1)}, bf16[5,16,64,128]{3,2,1,0:T(8,128)(2,1)S(1)}, bf16[1,5,16,64,128]{4,3,2,1,0:T(8,128)(2,1)S(1)}, bf16[320,640]{1,0:T(8,128)(2,1)S(1)}) custom-call(bf16[16,4,5,64,128]{4,3,2,1,0:T(8,128)(2,1)} %bitcast.6, bf16[16,4,5,64,128]{4,3,2,1,0:T(8,128)(2,1)} %bitcast.7, bf16[64,192]{1,0:T(8,128)(2,1)} %bitcast.8, ...), custom_call_target="tpu_custom_call" | custom-call | tf_op jit(solution)/shard_map/exchange/pallas_call | solution.py:396
  346.8 2.4 finish.1

commit v4 on v3

--- a/solution.py
+++ b/solution.py
@@ -243,18 +243,31 @@
                 crossed = jnp.dot(inv_ref[1, r], block, preferred_element_type=jnp.float32)
                 reply[slot, r, :, col] = (direct - turn(crossed, sign)).astype(jnp.bfloat16)
 
+        ending = slot == slots - 1
+
+        def answer(peer, r):
+            rows = pl.ds(pl.multiple_of(peer * local, local), local)
+            pltpu.make_async_remote_copy(
+                src_ref=reply.at[slot, r, rows, :],
+                dst_ref=back.at[slot, r, me],
+                send_sem=back_send.at[0],
+                recv_sem=back_recv.at[slot, r],
+                device_id={"energy": peer},
+                device_id_type=MESH,
+            ).start()
+
+        @pl.when(jnp.logical_and(ending, me > 0))
+        def _():
+            for r in range(radix):
+                answer(0, r)
+
         for r in range(radix):
             def ship(step, carry, r=r):
                 peer = partner(step)
-                rows = pl.ds(pl.multiple_of(peer * local, local), local)
-                pltpu.make_async_remote_copy(
-                    src_ref=reply.at[slot, r, rows, :],
-                    dst_ref=back.at[slot, r, me],
-                    send_sem=back_send.at[0],
-                    recv_sem=back_recv.at[slot, r],
-                    device_id={"energy": peer},
-                    device_id_type=MESH,
-                ).start()
+
+                @pl.when(jnp.logical_or(jnp.logical_not(ending), peer > 0))
+                def _():
+                    answer(peer, r)
                 return carry
 
             lax.fori_loop(0, peers - 1, ship, 0)
@@ -342,7 +355,7 @@
     slots, local, orbitals, _ = own_ref.shape
     sides = near_ref.shape[0] if weights.shape[1] > slots * orbitals else 0
     last = out_hbm.shape[1] - 1
-    share = local // 2
+    share = local // 4
     copies = [
         pltpu.make_async_copy(
             done.at[r, pl.ds(half * share, share)],
@@ -350,11 +363,11 @@
             copy_sem.at[r, half],
         )
         for r in range(last)
-        for half in range(2)
+        for half in range(4)
     ]
     for copy in copies:
         copy.start()
-    for half in range(2):
+    for half in range(4):
         for first in range(half * share, (half + 1) * share, 2):
             pairs = []
             for e in (first, first + 1):
@@ -429,7 +442,7 @@
         in_specs=[pl.BlockSpec(memory_space=pl.ANY), vmem, vmem, vmem],
         out_specs=pl.BlockSpec(memory_space=pltpu.HBM),
         scratch_shapes=[
-            pltpu.VMEM((local, slots, orbitals, cols), bf16), dma((kept, 2)), dma((2,)),
+            pltpu.VMEM((local, slots, orbitals, cols), bf16), dma((kept, 4)), dma((4,)),
         ],
         compiler_params=pltpu.CompilerParams(vmem_limit_bytes=16 * 1024 * 1024),
         name="finish",

time: 350 us -> 349 us (level); the launches traced: 349 us -> 344 us
  Pallas kernels: 349 us -> 344 us
    pallas_call x1, Pallas kernels: 347 us -> 341 us  [shards(): pl.pallas_call(functools.partial(exchange_kernel, peers, rows, radix), ou...]
where the time goes in v4:
time: 349 us; the launch traced here: 344 us
  Pallas kernels  344 us (99%)
    pallas_call x1, Pallas kernels, shards(): pl.pallas_call(functools.partial(exchange_kernel, peers, rows, radix), ou...  341 us

profile of v4, /device:TPU:0, one launch (start us, length us, event | category | flops | bytes accessed | tf_op | source)
XLA Modules:
  0.0 343.9 jit_solution(13266557605739629155)
XLA Ops:
  0.0 341.4 %exchange.1 = (bf16[3,16,5,64,128]{4,3,2,1,0:T(8,128)(2,1)S(1)}, bf16[5,16,64,128]{3,2,1,0:T(8,128)(2,1)S(1)}, bf16[1,5,16,64,128]{4,3,2,1,0:T(8,128)(2,1)S(1)}, bf16[320,640]{1,0:T(8,128)(2,1)S(1)}) custom-call(bf16[16,4,5,64,128]{4,3,2,1,0:T(8,128)(2,1)} %bitcast.6, bf16[16,4,5,64,128]{4,3,2,1,0:T(8,128)(2,1)} %bitcast.7, bf16[64,192]{1,0:T(8,128)(2,1)} %bitcast.8, ...), custom_call_target="tpu_custom_call" | custom-call | tf_op jit(solution)/shard_map/exchange/pallas_call | solution.py:409
  341.4 2.5 finish.1

commit v5 on v4

--- a/solution.py
+++ b/solution.py
@@ -357,13 +357,7 @@
     last = out_hbm.shape[1] - 1
     share = local // 4
     copies = [
-        pltpu.make_async_copy(
-            done.at[r, pl.ds(half * share, share)],
-            out_hbm.at[pl.ds(half * share, share), r],
-            copy_sem.at[r, half],
-        )
-        for r in range(last)
-        for half in range(4)
+        pltpu.make_async_copy(done.at[r], out_hbm.at[:, r], copy_sem.at[r]) for r in range(last)
     ]
     for copy in copies:
         copy.start()
@@ -442,7 +436,7 @@
         in_specs=[pl.BlockSpec(memory_space=pl.ANY), vmem, vmem, vmem],
         out_specs=pl.BlockSpec(memory_space=pltpu.HBM),
         scratch_shapes=[
-            pltpu.VMEM((local, slots, orbitals, cols), bf16), dma((kept, 4)), dma((4,)),
+            pltpu.VMEM((local, slots, orbitals, cols), bf16), dma((kept,)), dma((4,)),
         ],
         compiler_params=pltpu.CompilerParams(vmem_limit_bytes=16 * 1024 * 1024),
         name="finish",

time: 349 us -> 348 us (level)
  no operation moved by 1% of the time
where the time goes in v5:
time: 348 us; the launch traced here: 344 us
  Pallas kernels  344 us (99%)
    pallas_call x1, Pallas kernels, shards(): pl.pallas_call(functools.partial(exchange_kernel, peers, rows, radix), ou...  341 us

profile of v5, /device:TPU:0, one launch (start us, length us, event | category | flops | bytes accessed | tf_op | source)
XLA Modules:
  0.0 343.9 jit_solution(1529870569063151728)
XLA Ops:
  0.0 341.4 %exchange.1 = (bf16[3,16,5,64,128]{4,3,2,1,0:T(8,128)(2,1)S(1)}, bf16[5,16,64,128]{3,2,1,0:T(8,128)(2,1)S(1)}, bf16[1,5,16,64,128]{4,3,2,1,0:T(8,128)(2,1)S(1)}, bf16[320,640]{1,0:T(8,128)(2,1)S(1)}) custom-call(bf16[16,4,5,64,128]{4,3,2,1,0:T(8,128)(2,1)} %bitcast.6, bf16[16,4,5,64,128]{4,3,2,1,0:T(8,128)(2,1)} %bitcast.7, bf16[64,192]{1,0:T(8,128)(2,1)} %bitcast.8, ...), custom_call_target="tpu_custom_call" | custom-call | tf_op jit(solution)/shard_map/exchange/pallas_call | solution.py:403
  341.4 2.4 finish.1
